TPU v7x, 256 devices: a whole 4x4x8 slice. The times are simulated.
256 devices in a mesh: tile: 128 (over z_hi, x, y, core), member: 2 (over z_lo).
Axes of the slice: x: 4, y: 4, z: 8 (z_hi: 4, z_lo: 2; z = z_hi * 2 + z_lo), core: 2. Of those that a mesh axis runs over, the one named last changes fastest.
Arguments:
- fields: bfloat16 [2, 128, 2, 32, 32, 128], P('member', 'tile'), may hold values from -6 to 6
- cotangent: bfloat16 [2, 128, 2, 32, 32, 128], P('member', 'tile'), may hold values from -6 to 6
- edge_map: int32 [128, 4, 2], P('tile'), may hold values from 0 to 3, as said below
- w_first: bfloat16 [3, 3, 128, 128], replicated, may hold values from -0.1875 to 0.1875
- b_first: float32 [128], replicated, may hold values from -3 to 3
- w_second: bfloat16 [3, 3, 128, 128], replicated, may hold values from -0.1875 to 0.1875
- b_second: float32 [128], replicated, may hold values from -3 to 3
Outputs:
- response: bfloat16 [2, 128, 2, 32, 32, 128], P('member', 'tile')
- field_grad: bfloat16 [2, 128, 2, 32, 32, 128], P('member', 'tile')
- first_kernel_grad: float32 [3, 3, 128, 128], replicated
- first_bias_grad: float32 [128], replicated
- second_kernel_grad: float32 [3, 3, 128, 128], replicated
- second_bias_grad: float32 [128], replicated
Inputs may be any that keep to these rules, and one draw needn't show every extreme that they name: Each tile t is its own grid turned by r quarter turns: edge_map[t, g, 0] = (g - r) mod 4, and edge_map[t, g, 1] is 1 exactly when r = 2, or r = 1 and g is even, or r = 3 and g is odd.
All inputs are finite; a program needn't handle non-finite values.
Results may differ from a plain program's by a relative error of at most 0.0065.
Values may be sent and summed in bfloat16 or wider, within the bound.
A program may use at most 64 MiB of HBM per device.

v0:
```python
import jax
import jax.numpy as jnp
from jax import lax
from jax.sharding import PartitionSpec as P

ROW_TILES = 8
ROOT_HALF = 0.7071067811865476
INV_ROOT_TAU = 0.3989422804014327


def shifted(value, axis, steps):
    count = lax.axis_size(axis)
    pairs = [(source, (source + steps) % count) for source in range(count)]
    return lax.ppermute(value, axis, pairs)


def gelu_value(inputs):
    return 0.5 * inputs * (1.0 + jax.scipy.special.erf(inputs * ROOT_HALF))


def gelu_slope(inputs):
    return (
        0.5 * (1.0 + jax.scipy.special.erf(inputs * ROOT_HALF))
        + inputs * jnp.exp(-0.5 * inputs * inputs) * INV_ROOT_TAU
    )


def patches(padded):
    out_rows = padded.shape[-3] - 2
    out_cols = padded.shape[-2] - 2
    pieces = [
        padded[..., row_off : row_off + out_rows, col_off : col_off + out_cols, :]
        for row_off in range(3)
        for col_off in range(3)
    ]
    joined = jnp.concatenate(pieces, axis=-1)
    return joined.reshape(-1, joined.shape[-1])


def rim_strips(tile_data):
    return jnp.stack(
        [
            tile_data[..., 0, :, :],
            tile_data[..., :, -1, :],
            tile_data[..., -1, :, :],
            tile_data[..., :, 0, :],
        ],
        axis=-4,
    )


def orient(strips, chosen_ids, flip_ids):
    shaped_ids = chosen_ids.reshape(chosen_ids.shape + (1, 1, 1))
    shaped_flips = flip_ids.reshape(flip_ids.shape + (1, 1, 1))
    chosen = jnp.zeros_like(strips)
    for candidate in range(4):
        chosen = jnp.where(
            shaped_ids == candidate, jnp.expand_dims(strips[..., candidate, :, :, :], -4), chosen
        )
    flipped = chosen[..., ::-1, :]
    return jnp.where(shaped_flips == 1, flipped, chosen)


def assemble(tile_data, placed):
    top_rim = placed[..., 0, :, :, :]
    right_rim = placed[..., 1, :, :, :]
    bottom_rim = placed[..., 2, :, :, :]
    left_rim = placed[..., 3, :, :, :]
    kind = tile_data.dtype
    top_left = (
        0.5 * (top_rim[..., 0, :].astype(jnp.float32) + left_rim[..., 0, :].astype(jnp.float32))
    ).astype(kind)
    top_right = (
        0.5 * (top_rim[..., -1, :].astype(jnp.float32) + right_rim[..., 0, :].astype(jnp.float32))
    ).astype(kind)
    low_left = (
        0.5 * (bottom_rim[..., 0, :].astype(jnp.float32) + left_rim[..., -1, :].astype(jnp.float32))
    ).astype(kind)
    low_right = (
        0.5
        * (bottom_rim[..., -1, :].astype(jnp.float32) + right_rim[..., -1, :].astype(jnp.float32))
    ).astype(kind)
    top_row = jnp.concatenate([top_left[..., None, :], top_rim, top_right[..., None, :]], axis=-2)
    bottom_row = jnp.concatenate(
        [low_left[..., None, :], bottom_rim, low_right[..., None, :]], axis=-2
    )
    middle = jnp.concatenate(
        [left_rim[..., :, None, :], tile_data, right_rim[..., :, None, :]], axis=-2
    )
    return jnp.concatenate([top_row[..., None, :, :], middle, bottom_row[..., None, :, :]], axis=-3)


def fold_rims(grad_pad):
    interior = grad_pad[..., 1:-1, 1:-1, :]
    top_left = 0.5 * grad_pad[..., 0, 0, :]
    top_right = 0.5 * grad_pad[..., 0, -1, :]
    low_left = 0.5 * grad_pad[..., -1, 0, :]
    low_right = 0.5 * grad_pad[..., -1, -1, :]
    top_rim = grad_pad[..., 0, 1:-1, :].at[..., 0, :].add(top_left).at[..., -1, :].add(top_right)
    right_rim = (
        grad_pad[..., 1:-1, -1, :].at[..., 0, :].add(top_right).at[..., -1, :].add(low_right)
    )
    bottom_rim = (
        grad_pad[..., -1, 1:-1, :].at[..., 0, :].add(low_left).at[..., -1, :].add(low_right)
    )
    left_rim = grad_pad[..., 1:-1, 0, :].at[..., 0, :].add(top_left).at[..., -1, :].add(low_left)
    return (interior, jnp.stack([top_rim, right_rim, bottom_rim, left_rim], axis=-4))


def spread(interior, edge_grads):
    interior = interior.at[..., 0, :, :].add(edge_grads[..., 0, :, :, :])
    interior = interior.at[..., :, -1, :].add(edge_grads[..., 1, :, :, :])
    interior = interior.at[..., -1, :, :].add(edge_grads[..., 2, :, :, :])
    return interior.at[..., :, 0, :].add(edge_grads[..., 3, :, :, :])


def trade_rims(outgoing):
    offsets = (ROW_TILES, -1, -ROW_TILES, 1)
    received = []
    for direction in range(4):
        received.append(shifted(outgoing[(direction + 2) % 4], "tile", offsets[direction]))
    return jnp.stack(received)


def trade_grads(outgoing):
    offsets = (ROW_TILES, -1, -ROW_TILES, 1)
    received = []
    for direction in range(4):
        received.append(
            shifted(
                outgoing[(direction + 2) % 4].astype(jnp.bfloat16), "tile", offsets[direction]
            ).astype(jnp.float32)
        )
    return jnp.stack(received)


def pad_tile(tile_data, tables):
    side_ids, flip_marks, inverse, inverse_marks = tables
    outgoing = orient(rim_strips(tile_data), side_ids, flip_marks)
    incoming = trade_rims(outgoing)
    return assemble(tile_data, orient(incoming, inverse, inverse_marks))


def unpad_tile(grad_pad, tables):
    side_ids, flip_marks, inverse, inverse_marks = tables
    interior, placed = fold_rims(grad_pad)
    outgoing = orient(placed, side_ids, flip_marks)
    incoming = trade_grads(outgoing)
    return spread(interior, orient(incoming, inverse, inverse_marks))


def apply_cat(padded, weights_cat, out_rows, out_cols):
    product = jnp.dot(patches(padded), weights_cat, preferred_element_type=jnp.float32)
    return product.reshape(padded.shape[0], out_rows, out_cols, -1)


def forward_conv(tile_data, weights_cat, tables):
    tile_side = tile_data.shape[1]
    padded = pad_tile(tile_data, tables)
    result = apply_cat(padded, weights_cat, tile_side, tile_side)
    return (result, padded)


def back_conv(grad_data, weights_flip):
    tile_side = grad_data.shape[1]
    zero_pad = jnp.pad(grad_data, ((0, 0), (2, 2), (2, 2), (0, 0)))
    return apply_cat(zero_pad, weights_flip, tile_side + 2, tile_side + 2)


def kernel_term(padded, grad_data):
    channels = grad_data.shape[-1]
    total = lax.dot_general(
        patches(padded),
        grad_data.reshape(-1, channels),
        (((0,), (0,)), ((), ())),
        preferred_element_type=jnp.float32,
    )
    return total.reshape(3, 3, channels, channels)


def per_device(fields, cotangent, edge_map, w_first, b_first, w_second, b_second):
    frames, tile_side, channels = (fields.shape[2], fields.shape[3], fields.shape[5])
    source = fields.reshape(fields.shape[2:])
    upstream = cotangent.reshape(cotangent.shape[2:])
    side_ids = edge_map[0, :, 0]
    flip_marks = edge_map[0, :, 1]
    directions = jnp.arange(4, dtype=jnp.int32)
    inverse = jnp.sum(directions[None, :] * (side_ids[None, :] == directions[:, None]), axis=1)
    inverse_marks = jnp.take(flip_marks, inverse)
    tables = (side_ids, flip_marks, inverse, inverse_marks)
    first_cat = w_first.reshape(9 * channels, channels)
    second_cat = w_second.reshape(9 * channels, channels)
    first_flip = w_first[::-1, ::-1].transpose(0, 1, 3, 2).reshape(9 * channels, channels)
    second_flip = w_second[::-1, ::-1].transpose(0, 1, 3, 2).reshape(9 * channels, channels)
    norm_scale = float(
        lax.axis_size("tile") * lax.axis_size("member") * frames * tile_side * tile_side
    ) ** (-0.5)
    pre_one, pad_first = forward_conv(source, first_cat, tables)
    hidden_one = pre_one + b_first
    activity = gelu_value(hidden_one).astype(jnp.bfloat16)
    pre_two, pad_second = forward_conv(activity, second_cat, tables)
    hidden_two = pre_two + b_second
    response = gelu_value(hidden_two).astype(jnp.bfloat16)
    grad_second = (upstream.astype(jnp.float32) * gelu_slope(hidden_two)).astype(jnp.bfloat16)
    kernel_two = kernel_term(pad_second, grad_second)
    bias_two = jnp.sum(grad_second.astype(jnp.float32), axis=(0, 1, 2))
    grad_act = unpad_tile(back_conv(grad_second, second_flip), tables)
    grad_first = (grad_act * gelu_slope(hidden_one)).astype(jnp.bfloat16)
    kernel_one = kernel_term(pad_first, grad_first)
    bias_one = jnp.sum(grad_first.astype(jnp.float32), axis=(0, 1, 2))
    field_grad = unpad_tile(back_conv(grad_first, first_flip), tables).astype(jnp.bfloat16)
    kernel_one, bias_one, kernel_two, bias_two = lax.psum(
        (kernel_one, bias_one, kernel_two, bias_two), ("tile", "member")
    )
    return (
        response.reshape(fields.shape),
        field_grad.reshape(fields.shape),
        kernel_one * norm_scale,
        bias_one * norm_scale,
        kernel_two * norm_scale,
        bias_two * norm_scale,
    )


def solution(mesh):
    in_specs = (
        P("member", "tile", None, None, None, None),
        P("member", "tile", None, None, None, None),
        P("tile", None, None),
        P(),
        P(),
        P(),
        P(),
    )
    out_specs = (
        P("member", "tile", None, None, None, None),
        P("member", "tile", None, None, None, None),
        P(),
        P(),
        P(),
        P(),
    )
    return jax.shard_map(
        per_device, mesh=mesh, in_specs=in_specs, out_specs=out_specs, check_vma=False
    )
```

profile of v0, /device:TPU:2, one launch (start us, length us, event | category | flops | bytes accessed | tf_op | source)
XLA Modules:
  0.0 479.1 jit_solution(9307611065890658141)
XLA Ops:
  10.2 1.6 collective-permute-start.3
  11.8 3.5 collective-permute-start.2
  15.3 6.0 %collective-permute-start.1 = (bf16[2,32,128]{2,1,0:T(8,128)(2,1)S(1)}, bf16[2,32,128]{2,1,0:T(8,128)(2,1)S(1)}, u32[]{:S(2)}, u32[]{:S(2)}) collective-permute-start(bf16[2,32,128]{2,1,0:T(8,128)(2,1)S(1)} %get-tuple-element.401), channel_id=1, source_target_pairs={{0,240},{2,242},{4,244},{6,246},{8,248},{10,250},{12,252},{14,254}... | collective-permute-start | bytes 49160 | tf_op jit(solution)/shard_map/ppermute | solution.py:14
  36.3 3.8 collective-permute-start.6
  40.0 6.2 %collective-permute-start.5 = (bf16[2,32,128]{2,1,0:T(8,128)(2,1)S(1)}, bf16[2,32,128]{2,1,0:T(8,128)(2,1)S(1)}, u32[]{:S(2)}, u32[]{:S(2)}) collective-permute-start(bf16[2,32,128]{2,1,0:T(8,128)(2,1)S(1)} %get-tuple-element.391), channel_id=1, source_target_pairs={{0,240},{2,242},{4,244},{6,246},{8,248},{10,250},{12,252},{14,254}... | collective-permute-start | bytes 49160 | tf_op jit(solution)/shard_map/ppermute | solution.py:14
  46.2 1.9 constant_dynamic-update-slice_fusion.18
  50.0 1.9 constant_dynamic-update-slice_fusion.15
  56.3 6.7 %copy.180 = bf16[1152,2048]{1,0:T(8,128)(2,1)} copy(bf16[1152,2048]{0,1:T(8,128)(2,1)} %bitcast.102) | data formatting | bytes 9437184 | tf_op jit(solution)/shard_map/dot_general | solution.py:172
  66.4 4.8 %copy.182 = bf16[2,32,32,1152]{3,2,1,0:T(8,128)(2,1)} copy(bf16[2,32,32,1152]{3,1,0,2:T(8,128)(2,1)S(1)} %slice_dynamic-update-slice_fusion) | data formatting | bytes 9437184 | tf_op jit(solution)/shard_map/concatenate | solution.py:36
  71.3 2.5 convert_reduce_fusion
  76.5 2.3 fusion.2
  80.7 6.7 %copy.183 = bf16[1152,2048]{1,0:T(8,128)(2,1)} copy(bf16[1152,2048]{0,1:T(8,128)(2,1)} %bitcast.263) | data formatting | bytes 9437184 | tf_op jit(solution)/shard_map/dot_general | solution.py:172
  97.1 3.8 collective-permute-start.10
  100.8 6.0 %collective-permute-start.9 = (bf16[2,32,128]{2,1,0:T(8,128)(2,1)S(1)}, bf16[2,32,128]{2,1,0:T(8,128)(2,1)S(1)}, u32[]{:S(2)}, u32[]{:S(2)}) collective-permute-start(bf16[2,32,128]{2,1,0:T(8,128)(2,1)S(1)} %get-tuple-element.381), channel_id=1, source_target_pairs={{0,240},{2,242},{4,244},{6,246},{8,248},{10,250},{12,252},{14,254}... | collective-permute-start | bytes 49160 | tf_op jit(solution)/shard_map/ppermute | solution.py:14
  106.9 4.6 fusion.86
  117.4 2.1 fusion
  119.7 73.3 %all-reduce.2 = (f32[128]{0:T(128)S(1)}, f32[128]{0:T(128)S(1)}) all-reduce(f32[128]{0:T(128)S(1)} %get-tuple-element.318, f32[128]{0:T(128)S(1)} %copy-done.40), channel_id=1, replica_groups=mesh['tile'=128,'member'=2] {'tile','member'}, use_global_device_ids=true, to_apply=%region_3.4 | all-reduce | flops 256 | bytes 2048 | tf_op jit(solution)/shard_map/psum | solution.py:212
  194.1 2.3 collective-permute-start.15
  196.4 3.5 collective-permute-start.14
  199.9 5.4 %collective-permute-start.13 = (bf16[2,32,128]{2,1,0:T(8,128)(2,1)S(1)}, bf16[2,32,128]{2,1,0:T(8,128)(2,1)S(1)}, u32[]{:S(2)}, u32[]{:S(2)}) collective-permute-start(bf16[2,32,128]{2,1,0:T(8,128)(2,1)S(1)} %get-tuple-element.377), channel_id=1, source_target_pairs={{0,240},{2,242},{4,244},{6,246},{8,248},{10,250},{12,252},{14,254}... | collective-permute-start | bytes 49160 | tf_op jit(solution)/shard_map/ppermute | solution.py:14
  205.3 4.5 fusion.85
  212.8 255.2 %all-reduce.6.cloned.1.call-done = (f32[3,3,128,128]{3,2,1,0:T(8,128)}, f32[3,3,128,128]{3,2,1,0:T(8,128)}) async-done(((f32[3,3,128,128]{3,2,1,0:T(8,128)}, f32[3,3,128,128]{3,2,1,0:T(8,128)}), (f32[3,3,128,128]{3,2,1,0:T(8,128)}, f32[3,3,128,128]{3,2,1,0:T(8,128)})) %all-reduce.6.cloned.1.call-update) | async-done | bytes 1179664 | tf_op jit(solution)/shard_map/psum | solution.py:212
  468.0 1.9 broadcast_multiply_fusion.1
  469.9 1.9 broadcast_multiply_fusion
  (281 shorter events, 50.7 us)
Async XLA Ops:
  7.2 460.8 %all-reduce.6.cloned.1.call-start = ((), (), s32[]{:S(2)}) async-start(), calls=%async_computation | async-start | bytes 2359296 | tf_op jit(solution)/shard_map/psum | solution.py:212
  10.1 16.6 %collective-permute-start = (bf16[2,32,128]{2,1,0:T(8,128)(2,1)S(1)}, bf16[2,32,128]{2,1,0:T(8,128)(2,1)S(1)}, u32[]{:S(2)}, u32[]{:S(2)}) collective-permute-start(bf16[2,32,128]{2,1,0:T(8,128)(2,1)S(1)} %get-tuple-element.398), channel_id=1, source_target_pairs={{0,2},{2,4},{4,6},{6,8},{8,10},{10,12},{12,14},{14,16},{16,18},{18... | collective-permute-start | bytes 49160 | tf_op jit(solution)/shard_map/ppermute | solution.py:14
  10.2 16.5 %collective-permute-start.3 = (bf16[2,32,128]{2,1,0:T(8,128)(2,1)S(1)}, bf16[2,32,128]{2,1,0:T(8,128)(2,1)S(1)}, u32[]{:S(2)}, u32[]{:S(2)}) collective-permute-start(bf16[2,32,128]{2,1,0:T(8,128)(2,1)S(1)} %get-tuple-element.399), channel_id=1, source_target_pairs={{0,16},{2,18},{4,20},{6,22},{8,24},{10,26},{12,28},{14,30},{16,32}... | collective-permute-start | bytes 49160 | tf_op jit(solution)/shard_map/ppermute | solution.py:14
  11.8 15.0 %collective-permute-start.2 = (bf16[2,32,128]{2,1,0:T(8,128)(2,1)S(1)}, bf16[2,32,128]{2,1,0:T(8,128)(2,1)S(1)}, u32[]{:S(2)}, u32[]{:S(2)}) collective-permute-start(bf16[2,32,128]{2,1,0:T(8,128)(2,1)S(1)} %get-tuple-element.400), channel_id=1, source_target_pairs={{0,254},{2,0},{4,2},{6,4},{8,6},{10,8},{12,10},{14,12},{16,14},{18... | collective-permute-start | bytes 49160 | tf_op jit(solution)/shard_map/ppermute | solution.py:14
  15.3 11.5 %collective-permute-start.1 = (bf16[2,32,128]{2,1,0:T(8,128)(2,1)S(1)}, bf16[2,32,128]{2,1,0:T(8,128)(2,1)S(1)}, u32[]{:S(2)}, u32[]{:S(2)}) collective-permute-start(bf16[2,32,128]{2,1,0:T(8,128)(2,1)S(1)} %get-tuple-element.401), channel_id=1, source_target_pairs={{0,240},{2,242},{4,244},{6,246},{8,248},{10,250},{12,252},{14,254}... | collective-permute-start | bytes 49160 | tf_op jit(solution)/shard_map/ppermute | solution.py:14
  22.8 40.4 %copy-start.16 = (pred[4]{0:T(512)(128)(4,1)}, pred[4]{0:T(512)(128)(4,1)S(1)}, u32[]{:S(2)}) copy-start(pred[4]{0:T(512)(128)(4,1)S(1)} %get-tuple-element.433) | copy-start | bytes 16
  36.1 27.0 %collective-permute-start.4 = (bf16[2,32,128]{2,1,0:T(8,128)(2,1)S(1)}, bf16[2,32,128]{2,1,0:T(8,128)(2,1)S(1)}, u32[]{:S(2)}, u32[]{:S(2)}) collective-permute-start(bf16[2,32,128]{2,1,0:T(8,128)(2,1)S(1)} %get-tuple-element.388), channel_id=1, source_target_pairs={{0,2},{2,4},{4,6},{6,8},{8,10},{10,12},{12,14},{14,16},{16,18},{18... | collective-permute-start | bytes 49160 | tf_op jit(solution)/shard_map/ppermute | solution.py:14
  36.2 26.9 %collective-permute-start.7 = (bf16[2,32,128]{2,1,0:T(8,128)(2,1)S(1)}, bf16[2,32,128]{2,1,0:T(8,128)(2,1)S(1)}, u32[]{:S(2)}, u32[]{:S(2)}) collective-permute-start(bf16[2,32,128]{2,1,0:T(8,128)(2,1)S(1)} %get-tuple-element.389), channel_id=1, source_target_pairs={{0,16},{2,18},{4,20},{6,22},{8,24},{10,26},{12,28},{14,30},{16,32}... | collective-permute-start | bytes 49160 | tf_op jit(solution)/shard_map/ppermute | solution.py:14
  36.3 26.8 %collective-permute-start.6 = (bf16[2,32,128]{2,1,0:T(8,128)(2,1)S(1)}, bf16[2,32,128]{2,1,0:T(8,128)(2,1)S(1)}, u32[]{:S(2)}, u32[]{:S(2)}) collective-permute-start(bf16[2,32,128]{2,1,0:T(8,128)(2,1)S(1)} %get-tuple-element.390), channel_id=1, source_target_pairs={{0,254},{2,0},{4,2},{6,4},{8,6},{10,8},{12,10},{14,12},{16,14},{18... | collective-permute-start | bytes 49160 | tf_op jit(solution)/shard_map/ppermute | solution.py:14
  40.0 23.0 %collective-permute-start.5 = (bf16[2,32,128]{2,1,0:T(8,128)(2,1)S(1)}, bf16[2,32,128]{2,1,0:T(8,128)(2,1)S(1)}, u32[]{:S(2)}, u32[]{:S(2)}) collective-permute-start(bf16[2,32,128]{2,1,0:T(8,128)(2,1)S(1)} %get-tuple-element.391), channel_id=1, source_target_pairs={{0,240},{2,242},{4,244},{6,246},{8,248},{10,250},{12,252},{14,254}... | collective-permute-start | bytes 49160 | tf_op jit(solution)/shard_map/ppermute | solution.py:14
  96.9 15.9 %collective-permute-start.8 = (bf16[2,32,128]{2,1,0:T(8,128)(2,1)S(1)}, bf16[2,32,128]{2,1,0:T(8,128)(2,1)S(1)}, u32[]{:S(2)}, u32[]{:S(2)}) collective-permute-start(bf16[2,32,128]{2,1,0:T(8,128)(2,1)S(1)} %get-tuple-element.378), channel_id=1, source_target_pairs={{0,2},{2,4},{4,6},{6,8},{8,10},{10,12},{12,14},{14,16},{16,18},{18... | collective-permute-start | bytes 49160 | tf_op jit(solution)/shard_map/ppermute | solution.py:14
  97.0 15.8 %collective-permute-start.11 = (bf16[2,32,128]{2,1,0:T(8,128)(2,1)S(1)}, bf16[2,32,128]{2,1,0:T(8,128)(2,1)S(1)}, u32[]{:S(2)}, u32[]{:S(2)}) collective-permute-start(bf16[2,32,128]{2,1,0:T(8,128)(2,1)S(1)} %get-tuple-element.379), channel_id=1, source_target_pairs={{0,16},{2,18},{4,20},{6,22},{8,24},{10,26},{12,28},{14,30},{16,32}... | collective-permute-start | bytes 49160 | tf_op jit(solution)/shard_map/ppermute | solution.py:14
  97.1 15.8 %collective-permute-start.10 = (bf16[2,32,128]{2,1,0:T(8,128)(2,1)S(1)}, bf16[2,32,128]{2,1,0:T(8,128)(2,1)S(1)}, u32[]{:S(2)}, u32[]{:S(2)}) collective-permute-start(bf16[2,32,128]{2,1,0:T(8,128)(2,1)S(1)} %get-tuple-element.380), channel_id=1, source_target_pairs={{0,254},{2,0},{4,2},{6,4},{8,6},{10,8},{12,10},{14,12},{16,14},{18... | collective-permute-start | bytes 49160 | tf_op jit(solution)/shard_map/ppermute | solution.py:14
  100.8 12.0 %collective-permute-start.9 = (bf16[2,32,128]{2,1,0:T(8,128)(2,1)S(1)}, bf16[2,32,128]{2,1,0:T(8,128)(2,1)S(1)}, u32[]{:S(2)}, u32[]{:S(2)}) collective-permute-start(bf16[2,32,128]{2,1,0:T(8,128)(2,1)S(1)} %get-tuple-element.381), channel_id=1, source_target_pairs={{0,240},{2,242},{4,244},{6,246},{8,248},{10,250},{12,252},{14,254}... | collective-permute-start | bytes 49160 | tf_op jit(solution)/shard_map/ppermute | solution.py:14
  117.4 76.2 %copy-start.35 = (f32[2,1,1,128]{3,1,2,0:T(1,128)S(1)}, f32[2,1,1,128]{3,1,2,0:T(1,128)}, u32[]{:S(2)}) copy-start(f32[2,1,1,128]{3,1,2,0:T(1,128)} %copy-done.34) | copy-start | bytes 3076
  117.4 76.3 %copy-start.23 = (pred[4]{0:T(512)(128)(4,1)S(1)}, pred[4]{0:T(512)(128)(4,1)}, u32[]{:S(2)}) copy-start(pred[4]{0:T(512)(128)(4,1)} %copy-done.22) | copy-start | bytes 16
  117.4 76.3 %copy-start.25 = (pred[4]{0:T(512)(128)(4,1)S(1)}, pred[4]{0:T(512)(128)(4,1)}, u32[]{:S(2)}) copy-start(pred[4]{0:T(512)(128)(4,1)} %copy-done.24) | copy-start | bytes 16
  117.4 76.3 %copy-start.27 = (pred[4]{0:T(512)(128)(4,1)S(1)}, pred[4]{0:T(512)(128)(4,1)}, u32[]{:S(2)}) copy-start(pred[4]{0:T(512)(128)(4,1)} %copy-done.26) | copy-start | bytes 16
  117.4 76.3 %copy-start.29 = (pred[4]{0:T(512)(128)(4,1)S(1)}, pred[4]{0:T(512)(128)(4,1)}, u32[]{:S(2)}) copy-start(pred[4]{0:T(512)(128)(4,1)} %copy-done.28) | copy-start | bytes 16
  117.4 76.5 %copy-start.33 = (pred[4]{0:T(512)(128)(4,1)S(1)}, pred[4]{0:T(512)(128)(4,1)}, u32[]{:S(2)}) copy-start(pred[4]{0:T(512)(128)(4,1)} %copy-done.32) | copy-start | bytes 16
  194.0 16.6 %collective-permute-start.12 = (bf16[2,32,128]{2,1,0:T(8,128)(2,1)S(1)}, bf16[2,32,128]{2,1,0:T(8,128)(2,1)S(1)}, u32[]{:S(2)}, u32[]{:S(2)}) collective-permute-start(bf16[2,32,128]{2,1,0:T(8,128)(2,1)S(1)} %get-tuple-element.374), channel_id=1, source_target_pairs={{0,2},{2,4},{4,6},{6,8},{8,10},{10,12},{12,14},{14,16},{16,18},{18... | collective-permute-start | bytes 49160 | tf_op jit(solution)/shard_map/ppermute | solution.py:14
  194.1 16.6 %collective-permute-start.15 = (bf16[2,32,128]{2,1,0:T(8,128)(2,1)S(1)}, bf16[2,32,128]{2,1,0:T(8,128)(2,1)S(1)}, u32[]{:S(2)}, u32[]{:S(2)}) collective-permute-start(bf16[2,32,128]{2,1,0:T(8,128)(2,1)S(1)} %get-tuple-element.375), channel_id=1, source_target_pairs={{0,16},{2,18},{4,20},{6,22},{8,24},{10,26},{12,28},{14,30},{16,32}... | collective-permute-start | bytes 49160 | tf_op jit(solution)/shard_map/ppermute | solution.py:14
  196.4 14.3 %collective-permute-start.14 = (bf16[2,32,128]{2,1,0:T(8,128)(2,1)S(1)}, bf16[2,32,128]{2,1,0:T(8,128)(2,1)S(1)}, u32[]{:S(2)}, u32[]{:S(2)}) collective-permute-start(bf16[2,32,128]{2,1,0:T(8,128)(2,1)S(1)} %get-tuple-element.376), channel_id=1, source_target_pairs={{0,254},{2,0},{4,2},{6,4},{8,6},{10,8},{12,10},{14,12},{16,14},{18... | collective-permute-start | bytes 49160 | tf_op jit(solution)/shard_map/ppermute | solution.py:14
  199.9 10.8 %collective-permute-start.13 = (bf16[2,32,128]{2,1,0:T(8,128)(2,1)S(1)}, bf16[2,32,128]{2,1,0:T(8,128)(2,1)S(1)}, u32[]{:S(2)}, u32[]{:S(2)}) collective-permute-start(bf16[2,32,128]{2,1,0:T(8,128)(2,1)S(1)} %get-tuple-element.377), channel_id=1, source_target_pairs={{0,240},{2,242},{4,244},{6,246},{8,248},{10,250},{12,252},{14,254}... | collective-permute-start | bytes 49160 | tf_op jit(solution)/shard_map/ppermute | solution.py:14
  (34 other events, 451.3 us)
Sparse Core Ops, SparseCore 0:
  210.8 257.1 all-reduce.5
where the time goes:
time: 489 us; the launch traced here: 479 us
  waiting for transfers between devices  255 us (52%)
  blocking collectives  73.3 us (15%)
  local copies, waits for them, and re-layouts  56.4 us (12%)
  starting transfers between devices  42.5 us (9%)
  other arithmetic  18.3 us (4%)
  matrix products  17.4 us (4%)
  between operations  15.9 us (3%)
    psum x1, waiting for transfers between devices, per_device(): lax.psum((kernel_one, bias_one, kernel_two, bias_two), ('tile', 'member'))  255 us
    psum x1, blocking collectives, per_device(): lax.psum((kernel_one, bias_one, kernel_two, bias_two), ('tile', 'member'))  73.3 us
    ppermute x16, starting transfers between devices, shifted(): return lax.ppermute(value, axis, pairs)  42.5 us
    unnamed x134, local copies, waits for them, and re-layouts  23.3 us
    dot_general x2, local copies, waits for them, and re-layouts, kernel_term(): lax.dot_general(patches(padded), grad_data.reshape(-1, channels), (((0,),...  13.4 us
  transfers between devices with their start and end apart: 17, of which 1 were waited for; matrix products, arithmetic and copies ran while one was open for 7% of the time, Pallas kernels for 0%

commit v1 on v0

--- a/solution.py
+++ b/solution.py
@@ -210,7 +210,7 @@
     bias_one = jnp.sum(grad_first.astype(jnp.float32), axis=(0, 1, 2))
     field_grad = unpad_tile(back_conv(grad_first, first_flip), tables).astype(jnp.bfloat16)
     kernel_one, bias_one, kernel_two, bias_two = lax.psum(
-        (kernel_one, bias_one, kernel_two, bias_two), ("tile", "member")
+        lax.psum((kernel_one, bias_one, kernel_two, bias_two), "tile"), "member"
     )
     return (
         response.reshape(fields.shape),

time: 489 us -> 1480 us (3.03)
  waiting for transfers between devices: 255 us -> 998 us
  blocking collectives: 73.3 us -> 320 us
    psum x1 -> x2, waiting for transfers between devices: 255 us -> 998 us  [the longest x1 926 us: per_device(): lax.psum((kernel_one, bias_one, kernel_two, bias_two), 'tile')]
    psum x1 -> x2, blocking collectives: 73.3 us -> 320 us  [the longest x1 315 us: per_device(): lax.psum((kernel_one, bias_one, kernel_two, bias_two), 'tile')]
  transfers between devices with their start and end apart: 17 -> 18, of which waited for: 1 -> 2; matrix products, arithmetic and copies ran while one was open for 7% -> 2% of each run, Pallas kernels for 0% -> 0%
where the time goes in v1:
time: 1480 us; the launch traced here: 1470 us
  waiting for transfers between devices  998 us (67%)
  blocking collectives  320 us (22%)
  local copies, waits for them, and re-layouts  56.4 us (4%)
  starting transfers between devices  41.2 us (3%)
  other arithmetic  18.3 us (1%)
  matrix products  17.4 us (1%)
  between operations  16 us (1%)
    psum x1, waiting for transfers between devices, per_device(): lax.psum((kernel_one, bias_one, kernel_two, bias_two), 'tile')  926 us
    psum x1, blocking collectives, per_device(): lax.psum((kernel_one, bias_one, kernel_two, bias_two), 'tile')  315 us
    psum x1, waiting for transfers between devices, per_device(): lax.psum(lax.psum((kernel_one, bias_one, kernel_two, bias_two), 'tile'),...  72 us
    ppermute x16, starting transfers between devices, shifted(): return lax.ppermute(value, axis, pairs)  41.1 us
  transfers between devices with their start and end apart: 18, of which 2 were waited for; matrix products, arithmetic and copies ran while one was open for 2% of the time, Pallas kernels for 0%

profile of v1, /device:TPU:2, one launch (start us, length us, event | category | flops | bytes accessed | tf_op | source)
XLA Modules:
  0.0 1466.6 jit_solution(12651013485872004654)
XLA Ops:
  11.8 3.5 collective-permute-start.2
  15.3 6.0 collective-permute-start.1
  36.3 3.8 collective-permute-start.6
  40.0 6.2 collective-permute-start.5
  46.2 1.9 constant_dynamic-update-slice_fusion.18
  50.0 1.9 constant_dynamic-update-slice_fusion.15
  56.3 6.7 copy.180
  66.4 4.8 copy.182
  71.2 2.5 convert_reduce_fusion
  76.5 2.3 fusion.2
  80.7 6.7 copy.183
  97.1 3.8 collective-permute-start.10
  100.8 6.0 collective-permute-start.9
  106.8 4.5 fusion.86
  117.4 2.1 fusion
  120.1 4.5 fusion.85
  125.0 3.8 collective-permute-start.14
  128.8 6.0 collective-permute-start.13
  134.8 314.7 %all-reduce.2 = (f32[128]{0:T(128)S(1)}, f32[128]{0:T(128)S(1)}) all-reduce(f32[128]{0:T(128)S(1)} %get-tuple-element.322, f32[128]{0:T(128)S(1)} %copy-done.40), channel_id=1, replica_groups=mesh['tile'=128,'member'=2] {'tile'}, use_global_device_ids=true, to_apply=%region_4.5 | all-reduce | flops 256 | bytes 2048 | tf_op jit(solution)/shard_map/psum | solution.py:213
  449.5 4.9 all-reduce.4
  456.0 925.7 %all-reduce.9.cloned.1.call-done = (f32[3,3,128,128]{3,2,1,0:T(8,128)}, f32[3,3,128,128]{3,2,1,0:T(8,128)}) async-done(((f32[3,3,128,128]{3,2,1,0:T(8,128)}, f32[3,3,128,128]{3,2,1,0:T(8,128)}), (f32[3,3,128,128]{3,2,1,0:T(8,128)}, f32[3,3,128,128]{3,2,1,0:T(8,128)})) %all-reduce.9.cloned.1.call-update) | async-done | bytes 1179664 | tf_op jit(solution)/shard_map/psum | solution.py:213
  1383.5 72.0 %all-reduce.11.cloned.1.call-done = (f32[3,3,128,128]{3,2,1,0:T(8,128)}, f32[3,3,128,128]{3,2,1,0:T(8,128)}) async-done(((f32[3,3,128,128]{3,2,1,0:T(8,128)}, f32[3,3,128,128]{3,2,1,0:T(8,128)}), (f32[3,3,128,128]{3,2,1,0:T(8,128)}, f32[3,3,128,128]{3,2,1,0:T(8,128)})) %all-reduce.11.cloned.1.call-update) | async-done | bytes 1179664 | tf_op jit(solution)/shard_map/psum | solution.py:212
  1455.5 1.9 broadcast_multiply_fusion.1
  1457.5 1.9 broadcast_multiply_fusion
  (285 shorter events, 52.4 us)
Async XLA Ops:
  7.2 1374.5 %all-reduce.9.cloned.1.call-start = ((), (), s32[]{:S(2)}) async-start(), calls=%async_computation | async-start | bytes 2359296 | tf_op jit(solution)/shard_map/psum | solution.py:213
  9.8 26.1 %copy-start.24 = (pred[4]{0:T(512)(128)(4,1)}, pred[4]{0:T(512)(128)(4,1)S(1)}, u32[]{:S(2)}) copy-start(pred[4]{0:T(512)(128)(4,1)S(1)} %get-tuple-element.432) | copy-start | bytes 16
  10.1 16.6 %collective-permute-start = (bf16[2,32,128]{2,1,0:T(8,128)(2,1)S(1)}, bf16[2,32,128]{2,1,0:T(8,128)(2,1)S(1)}, u32[]{:S(2)}, u32[]{:S(2)}) collective-permute-start(bf16[2,32,128]{2,1,0:T(8,128)(2,1)S(1)} %get-tuple-element.402), channel_id=1, source_target_pairs={{0,2},{2,4},{4,6},{6,8},{8,10},{10,12},{12,14},{14,16},{16,18},{18... | collective-permute-start | bytes 49160 | tf_op jit(solution)/shard_map/ppermute | solution.py:14
  10.2 16.5 %collective-permute-start.3 = (bf16[2,32,128]{2,1,0:T(8,128)(2,1)S(1)}, bf16[2,32,128]{2,1,0:T(8,128)(2,1)S(1)}, u32[]{:S(2)}, u32[]{:S(2)}) collective-permute-start(bf16[2,32,128]{2,1,0:T(8,128)(2,1)S(1)} %get-tuple-element.403), channel_id=1, source_target_pairs={{0,16},{2,18},{4,20},{6,22},{8,24},{10,26},{12,28},{14,30},{16,32}... | collective-permute-start | bytes 49160 | tf_op jit(solution)/shard_map/ppermute | solution.py:14
  11.8 15.0 %collective-permute-start.2 = (bf16[2,32,128]{2,1,0:T(8,128)(2,1)S(1)}, bf16[2,32,128]{2,1,0:T(8,128)(2,1)S(1)}, u32[]{:S(2)}, u32[]{:S(2)}) collective-permute-start(bf16[2,32,128]{2,1,0:T(8,128)(2,1)S(1)} %get-tuple-element.404), channel_id=1, source_target_pairs={{0,254},{2,0},{4,2},{6,4},{8,6},{10,8},{12,10},{14,12},{16,14},{18... | collective-permute-start | bytes 49160 | tf_op jit(solution)/shard_map/ppermute | solution.py:14
  15.3 11.5 collective-permute-start.1
  22.8 40.4 %copy-start.14 = (pred[4]{0:T(512)(128)(4,1)}, pred[4]{0:T(512)(128)(4,1)S(1)}, u32[]{:S(2)}) copy-start(pred[4]{0:T(512)(128)(4,1)S(1)} %get-tuple-element.436) | copy-start | bytes 16
  22.8 40.4 %copy-start.16 = (pred[4]{0:T(512)(128)(4,1)}, pred[4]{0:T(512)(128)(4,1)S(1)}, u32[]{:S(2)}) copy-start(pred[4]{0:T(512)(128)(4,1)S(1)} %get-tuple-element.437) | copy-start | bytes 16
  22.9 40.4 %copy-start.18 = (pred[4]{0:T(512)(128)(4,1)}, pred[4]{0:T(512)(128)(4,1)S(1)}, u32[]{:S(2)}) copy-start(pred[4]{0:T(512)(128)(4,1)S(1)} %get-tuple-element.438) | copy-start | bytes 16
  22.9 40.4 %copy-start.20 = (pred[4]{0:T(512)(128)(4,1)}, pred[4]{0:T(512)(128)(4,1)S(1)}, u32[]{:S(2)}) copy-start(pred[4]{0:T(512)(128)(4,1)S(1)} %get-tuple-element.439) | copy-start | bytes 16
  22.9 40.4 %copy-start.30 = (pred[4]{0:T(512)(128)(4,1)}, pred[4]{0:T(512)(128)(4,1)S(1)}, u32[]{:S(2)}) copy-start(pred[4]{0:T(512)(128)(4,1)S(1)} %get-tuple-element.435) | copy-start | bytes 16
  36.1 27.0 %collective-permute-start.4 = (bf16[2,32,128]{2,1,0:T(8,128)(2,1)S(1)}, bf16[2,32,128]{2,1,0:T(8,128)(2,1)S(1)}, u32[]{:S(2)}, u32[]{:S(2)}) collective-permute-start(bf16[2,32,128]{2,1,0:T(8,128)(2,1)S(1)} %get-tuple-element.392), channel_id=1, source_target_pairs={{0,2},{2,4},{4,6},{6,8},{8,10},{10,12},{12,14},{14,16},{16,18},{18... | collective-permute-start | bytes 49160 | tf_op jit(solution)/shard_map/ppermute | solution.py:14
  36.2 26.9 %collective-permute-start.7 = (bf16[2,32,128]{2,1,0:T(8,128)(2,1)S(1)}, bf16[2,32,128]{2,1,0:T(8,128)(2,1)S(1)}, u32[]{:S(2)}, u32[]{:S(2)}) collective-permute-start(bf16[2,32,128]{2,1,0:T(8,128)(2,1)S(1)} %get-tuple-element.393), channel_id=1, source_target_pairs={{0,16},{2,18},{4,20},{6,22},{8,24},{10,26},{12,28},{14,30},{16,32}... | collective-permute-start | bytes 49160 | tf_op jit(solution)/shard_map/ppermute | solution.py:14
  36.3 26.8 %collective-permute-start.6 = (bf16[2,32,128]{2,1,0:T(8,128)(2,1)S(1)}, bf16[2,32,128]{2,1,0:T(8,128)(2,1)S(1)}, u32[]{:S(2)}, u32[]{:S(2)}) collective-permute-start(bf16[2,32,128]{2,1,0:T(8,128)(2,1)S(1)} %get-tuple-element.394), channel_id=1, source_target_pairs={{0,254},{2,0},{4,2},{6,4},{8,6},{10,8},{12,10},{14,12},{16,14},{18... | collective-permute-start | bytes 49160 | tf_op jit(solution)/shard_map/ppermute | solution.py:14
  40.0 23.0 %collective-permute-start.5 = (bf16[2,32,128]{2,1,0:T(8,128)(2,1)S(1)}, bf16[2,32,128]{2,1,0:T(8,128)(2,1)S(1)}, u32[]{:S(2)}, u32[]{:S(2)}) collective-permute-start(bf16[2,32,128]{2,1,0:T(8,128)(2,1)S(1)} %get-tuple-element.395), channel_id=1, source_target_pairs={{0,240},{2,242},{4,244},{6,246},{8,248},{10,250},{12,252},{14,254}... | collective-permute-start | bytes 49160 | tf_op jit(solution)/shard_map/ppermute | solution.py:14
  96.9 15.9 %collective-permute-start.8 = (bf16[2,32,128]{2,1,0:T(8,128)(2,1)S(1)}, bf16[2,32,128]{2,1,0:T(8,128)(2,1)S(1)}, u32[]{:S(2)}, u32[]{:S(2)}) collective-permute-start(bf16[2,32,128]{2,1,0:T(8,128)(2,1)S(1)} %get-tuple-element.382), channel_id=1, source_target_pairs={{0,2},{2,4},{4,6},{6,8},{8,10},{10,12},{12,14},{14,16},{16,18},{18... | collective-permute-start | bytes 49160 | tf_op jit(solution)/shard_map/ppermute | solution.py:14
  97.0 15.8 %collective-permute-start.11 = (bf16[2,32,128]{2,1,0:T(8,128)(2,1)S(1)}, bf16[2,32,128]{2,1,0:T(8,128)(2,1)S(1)}, u32[]{:S(2)}, u32[]{:S(2)}) collective-permute-start(bf16[2,32,128]{2,1,0:T(8,128)(2,1)S(1)} %get-tuple-element.383), channel_id=1, source_target_pairs={{0,16},{2,18},{4,20},{6,22},{8,24},{10,26},{12,28},{14,30},{16,32}... | collective-permute-start | bytes 49160 | tf_op jit(solution)/shard_map/ppermute | solution.py:14
  97.1 15.8 %collective-permute-start.10 = (bf16[2,32,128]{2,1,0:T(8,128)(2,1)S(1)}, bf16[2,32,128]{2,1,0:T(8,128)(2,1)S(1)}, u32[]{:S(2)}, u32[]{:S(2)}) collective-permute-start(bf16[2,32,128]{2,1,0:T(8,128)(2,1)S(1)} %get-tuple-element.384), channel_id=1, source_target_pairs={{0,254},{2,0},{4,2},{6,4},{8,6},{10,8},{12,10},{14,12},{16,14},{18... | collective-permute-start | bytes 49160 | tf_op jit(solution)/shard_map/ppermute | solution.py:14
  100.8 12.0 collective-permute-start.9
  124.7 1330.9 %all-reduce.11.cloned.1.call-start = ((), (), s32[]{:S(2)}) async-start(), calls=%async_computation.1 | async-start | bytes 2359296 | tf_op jit(solution)/shard_map/psum | solution.py:212
  124.9 330.8 %collective-permute-start.12 = (bf16[2,32,128]{2,1,0:T(8,128)(2,1)S(1)}, bf16[2,32,128]{2,1,0:T(8,128)(2,1)S(1)}, u32[]{:S(2)}, u32[]{:S(2)}) collective-permute-start(bf16[2,32,128]{2,1,0:T(8,128)(2,1)S(1)} %get-tuple-element.378), channel_id=1, source_target_pairs={{0,2},{2,4},{4,6},{6,8},{8,10},{10,12},{12,14},{14,16},{16,18},{18... | collective-permute-start | bytes 49160 | tf_op jit(solution)/shard_map/ppermute | solution.py:14
  124.9 330.8 %collective-permute-start.15 = (bf16[2,32,128]{2,1,0:T(8,128)(2,1)S(1)}, bf16[2,32,128]{2,1,0:T(8,128)(2,1)S(1)}, u32[]{:S(2)}, u32[]{:S(2)}) collective-permute-start(bf16[2,32,128]{2,1,0:T(8,128)(2,1)S(1)} %get-tuple-element.379), channel_id=1, source_target_pairs={{0,16},{2,18},{4,20},{6,22},{8,24},{10,26},{12,28},{14,30},{16,32}... | collective-permute-start | bytes 49160 | tf_op jit(solution)/shard_map/ppermute | solution.py:14
  125.0 330.7 %collective-permute-start.14 = (bf16[2,32,128]{2,1,0:T(8,128)(2,1)S(1)}, bf16[2,32,128]{2,1,0:T(8,128)(2,1)S(1)}, u32[]{:S(2)}, u32[]{:S(2)}) collective-permute-start(bf16[2,32,128]{2,1,0:T(8,128)(2,1)S(1)} %get-tuple-element.380), channel_id=1, source_target_pairs={{0,254},{2,0},{4,2},{6,4},{8,6},{10,8},{12,10},{14,12},{16,14},{18... | collective-permute-start | bytes 49160 | tf_op jit(solution)/shard_map/ppermute | solution.py:14
  128.8 327.0 %collective-permute-start.13 = (bf16[2,32,128]{2,1,0:T(8,128)(2,1)S(1)}, bf16[2,32,128]{2,1,0:T(8,128)(2,1)S(1)}, u32[]{:S(2)}, u32[]{:S(2)}) collective-permute-start(bf16[2,32,128]{2,1,0:T(8,128)(2,1)S(1)} %get-tuple-element.381), channel_id=1, source_target_pairs={{0,240},{2,242},{4,244},{6,246},{8,248},{10,250},{12,252},{14,254}... | collective-permute-start | bytes 49160 | tf_op jit(solution)/shard_map/ppermute | solution.py:14
  (35 other events, 294.3 us)
Sparse Core Ops, SparseCore 0:
  124.8 1256.8 all-reduce.8
  1384.3 71.1 all-reduce.10
